TPU v7x, 32 devices: a whole 2x2x4 slice. The times are simulated.
32 devices in a mesh: prow: 4 (over y, x), pcol: 8 (over z, core).
Axes of the slice: x: 2, y: 2, z: 4, core: 2. Of those that a mesh axis runs over, the one named last changes fastest.
Arguments:
- diag_block: float32 [128, 128], replicated, may hold values from 0 to 1.03, as said below
- panel: float32 [8192, 128], P(('prow', 'pcol')), may hold values from -0.2 to 1.2
- slab: float32 [8192, 2048], P('prow', 'pcol'), may hold values from -6 to 6
Outputs:
- slab_next: float32 [8192, 2048], P('prow', 'pcol')
- panel_factor: float32 [8192, 128], P(('prow', 'pcol'))
Inputs may be any that keep to these rules, and one draw needn't show every extreme that they name: diag_block is symmetric positive definite.
All inputs are finite; a program needn't handle non-finite values.
Results may differ from a plain program's by a relative error of at most 0.00091.
Values may be sent and summed in bfloat16 or wider, within the bound.
No kernel may reach another device: no remote copies, remote signals or barrier semaphores. Data moves between devices by JAX's collectives and lax.ppermute only.
A program may use at most 64 MiB of HBM per device.

v0:
```python
import jax
import jax.numpy as jnp
from jax import lax
from jax.sharding import PartitionSpec as P


def spread_2(x, axis, root):
    mine = lax.axis_index(axis) == root
    return lax.psum(jnp.where(mine, x, jnp.zeros_like(x)), axis)


def solve_rows(factor_block, rows_given):
    return lax.linalg.triangular_solve(
        factor_block, rows_given, left_side=False, lower=True, transpose_a=True
    )


def pick_blocks(source, leading, spread, panel_width, blocks_here):
    pieces = [
        lax.dynamic_slice_in_dim(
            source, (leading + position * spread) * panel_width, panel_width, 0
        )
        for position in range(blocks_here)
    ]
    return jnp.concatenate(pieces, 0)


def per_device(diag_block, panel, slab):
    prows = lax.axis_size("prow")
    pcols = lax.axis_size("pcol")
    factor_block = jnp.linalg.cholesky(diag_block)
    panel_width = factor_block.shape[0]
    spread = pcols // prows
    column_index = lax.axis_index("pcol")
    leading = column_index // prows
    blocks_here = slab.shape[1] // panel_width
    solved_rows = solve_rows(factor_block, panel)
    row_factor = lax.all_gather(solved_rows.astype(jnp.bfloat16), "pcol", axis=0, tiled=True)
    candidate = pick_blocks(row_factor, leading, spread, panel_width, blocks_here)
    column_factor = spread_2(candidate, "prow", column_index % prows)
    product = lax.dot_general(
        row_factor, column_factor, (((1,), (1,)), ((), ())), preferred_element_type=jnp.float32
    )
    return (slab - product, solved_rows)


def solution(mesh):
    placed = (P(), P(("prow", "pcol"), None), P("prow", "pcol"))
    return jax.shard_map(
        per_device,
        mesh=mesh,
        in_specs=placed,
        out_specs=(P("prow", "pcol"), P(("prow", "pcol"), None)),
        check_vma=False,
    )
```

profile of v0, /device:TPU:0, one launch (start us, length us, event | category | flops | bytes accessed | tf_op | source)
XLA Modules:
  0.0 102.2 jit_solution(17557626038271125850)
XLA Ops:
  7.2 0.0 copy-start
  7.2 0.0 copy-start.1
  7.2 0.0 all-reduce.2.cloned.1.call-start
  7.3 1.1 %copy.5 = f32[128,128]{0,1:T(8,128)S(1)} copy(f32[128,128]{1,0:T(8,128)} %param.3) | data formatting | bytes 131072 | tf_op args[0]
  8.3 0.9 fusion.2
  9.2 11.7 %cholesky.16 = f32[128,128]{1,0:T(8,128)S(1)} custom-call(f32[128,128]{1,0:T(8,128)S(1)} %fusion.2), custom_call_target="Cholesky" | custom-call | tf_op jit(solution)/shard_map/jit(cholesky)/cholesky | solution.py:31
  20.9 0.6 compare_reduce_fusion
  21.6 0.7 fusion
  22.3 9.8 %custom-call.6 = f32[1,128,128]{1,2,0:T(8,128)S(1)} custom-call(f32[1,128,128]{2,1,0:T(8,128)S(1)} %fusion), custom_call_target="InvertDiagBlocksLowerTriangular" | custom-call | tf_op jit(solution)/shard_map/triangular_solve | solution.py:13
  32.1 0.0 copy-done
  32.1 0.3 fusion.3
  32.4 16.5 %all_gather.3 = bf16[2048,128]{0,1:T(8,128)(2,1)S(1)} all-gather(bf16[256,128]{0,1:T(8,128)(2,1)S(1)} %get-tuple-element.6), channel_id=1, replica_groups=mesh['prow'=4,'pcol'=8] {'pcol'}, dimensions={0}, use_global_device_ids=true | all-gather | bytes 589824 | tf_op jit(solution)/shard_map/all_gather | solution.py:38
  48.9 0.6 maximum_select_fusion
  49.6 0.0 all-reduce.2.cloned.1.call-update
  49.6 0.8 copy.6
  50.4 42.3 %all-reduce.2.cloned.1.call-done = bf16[256,128]{0,1:T(8,128)(2,1)} async-done(((bf16[256,128]{0,1:T(8,128)(2,1)}), bf16[256,128]{0,1:T(8,128)(2,1)}) %all-reduce.2.cloned.1.call-update) | async-done | bytes 65552 | tf_op jit(solution)/shard_map/psum | solution.py:9
  92.7 0.0 copy-done.1
  92.7 2.6 %convolution_subtract_fusion = f32[2048,256]{1,0:T(8,128)} fusion(f32[2048,256]{1,0:T(8,128)S(1)} %copy-done.1, bf16[2048,128]{0,1:T(8,128)(2,1)S(1)} %all_gather.3, bf16[256,128]{0,1:T(8,128)(2,1)} %all-reduce.2.cloned.1.call-done), kind=kOutput, calls=%fused_computation | convolution fusion | flops 134742016 | bytes 4784128 | tf_op jit(solution)/shard_map/dot_general | solution.py:41
  (2 shorter events, 0.1 us)
Async XLA Ops:
  7.2 24.9 %copy-start = (f32[256,128]{1,0:T(8,128)S(1)}, f32[256,128]{1,0:T(8,128)}, u32[]{:S(2)}) copy-start(f32[256,128]{1,0:T(8,128)} %param.4) | copy-start | bytes 393220
  7.2 85.5 %copy-start.1 = (f32[2048,256]{1,0:T(8,128)S(1)}, f32[2048,256]{1,0:T(8,128)}, u32[]{:S(2)}) copy-start(f32[2048,256]{1,0:T(8,128)} %param.5) | copy-start | bytes 6291460
  7.2 85.5 %all-reduce.2.cloned.1.call-start = ((), (), s32[]{:S(2)}) async-start(), calls=%async_computation | async-start | bytes 131072 | tf_op jit(solution)/shard_map/psum | solution.py:9
Sparse Core Ops, SparseCore 0:
  49.7 42.9 all-reduce.1
where the time goes:
time: 102 us
  waiting for transfers between devices  42.3 us (41%)
  other arithmetic  24.4 us (24%)
  blocking collectives  16.5 us (16%)
  between operations  14.1 us (14%)
  matrix products  2.93 us (3%)
  local copies, waits for them, and re-layouts  1.86 us (2%)
    psum x1, waiting for transfers between devices, spread_2(): return lax.psum(jnp.where(mine, x, jnp.zeros_like(x)), axis)  42.3 us
    all_gather x1, blocking collectives, per_device(): lax.all_gather(solved_rows.astype(jnp.bfloat16), 'pcol', axis=0, tiled=True)  16.5 us
    another operation x3, other arithmetic, per_device(): factor_block = jnp.linalg.cholesky(diag_block)  12.4 us
    another operation x2, other arithmetic, solve_rows(): lax.linalg.triangular_solve(factor_block, rows_given, left_side=False, lo...  10.5 us
    dot_general x1, matrix products, per_device(): lax.dot_general(row_factor, column_factor, (((1,), (1,)), ((), ())), pref...  2.62 us
  transfers between devices with their start and end apart: 1, of which 1 were waited for; matrix products, arithmetic and copies ran while one was open for 1% of the time, Pallas kernels for 0%

commit v1 on v0

--- a/solution.py
+++ b/solution.py
@@ -6,7 +6,7 @@
 
 def spread_2(x, axis, root):
     mine = lax.axis_index(axis) == root
-    return lax.psum(jnp.where(mine, x, jnp.zeros_like(x)), axis)
+    return jnp.sum(lax.all_gather(jnp.where(mine, x, jnp.zeros_like(x)), axis), axis=0)
 
 
 def solve_rows(factor_block, rows_given):

time: 102 us -> 54.4 us (0.53)
  waiting for transfers between devices: 42.3 us -> 0 us
  between operations: 14.1 us -> 0.76 us
  blocking collectives: 16.5 us -> 25.5 us
    psum x1 -> x0, waiting for transfers between devices: 42.3 us -> none  [spread_2(): return lax.psum(jnp.where(mine, x, jnp.zeros_like(x)), axis)]
    all_gather x0 -> x1, blocking collectives: none -> 9 us  [spread_2(): lax.all_gather(jnp.where(mine, x, jnp.zeros_like(x)), axis)]
  transfers between devices with their start and end apart: 1 -> 0, of which waited for: 1 -> 0; matrix products, arithmetic and copies ran while one was open for 1% -> 0% of each run, Pallas kernels for 0% -> 0%
where the time goes in v1:
time: 54.4 us; the launch traced here: 54.2 us
  blocking collectives  25.5 us (47%)
  other arithmetic  23.8 us (44%)
  local copies, waits for them, and re-layouts  2.1 us (4%)
  matrix products  2.1 us (4%)
  between operations  0.76 us (1%)
    all_gather x1, blocking collectives, per_device(): lax.all_gather(solved_rows.astype(jnp.bfloat16), 'pcol', axis=0, tiled=True)  16.5 us
    another operation x3, other arithmetic, per_device(): factor_block = jnp.linalg.cholesky(diag_block)  12.4 us
    another operation x2, other arithmetic, solve_rows(): lax.linalg.triangular_solve(factor_block, rows_given, left_side=False, lo...  10.5 us
    all_gather x1, blocking collectives, spread_2(): lax.all_gather(jnp.where(mine, x, jnp.zeros_like(x)), axis)  9 us
    unnamed x6, local copies, waits for them, and re-layouts  1.85 us
    dot_general x1, matrix products, per_device(): lax.dot_general(row_factor, column_factor, (((1,), (1,)), ((), ())), pref...  1.79 us

profile of v1, /device:TPU:0, one launch (start us, length us, event | category | flops | bytes accessed | tf_op | source)
XLA Modules:
  0.0 54.2 jit_solution(12004026883969294216)
XLA Ops:
  0.6 0.0 copy-start
  0.6 0.0 copy-start.1
  0.7 1.1 %copy.10 = f32[128,128]{0,1:T(8,128)S(1)} copy(f32[128,128]{1,0:T(8,128)} %param.3) | data formatting | bytes 131072 | tf_op args[0]
  1.8 0.9 %fusion.2 = f32[128,128]{1,0:T(8,128)S(1)} fusion(f32[128,128]{1,0:T(8,128)} %param.3, f32[128,128]{0,1:T(8,128)S(1)} %copy.10), kind=kLoop, calls=%fused_computation.7 | loop fusion | flops 32768 | bytes 196608 | tf_op jit(solution)/shard_map/jit(cholesky)/div | solution.py:31
  2.6 11.7 %cholesky.16 = f32[128,128]{1,0:T(8,128)S(1)} custom-call(f32[128,128]{1,0:T(8,128)S(1)} %fusion.2), custom_call_target="Cholesky" | custom-call | tf_op jit(solution)/shard_map/jit(cholesky)/cholesky | solution.py:31
  14.4 0.6 %compare_reduce_fusion = pred[]{:T(512)} fusion(f32[128]{0:T(128)S(1)} %select_reduce_fusion), kind=kLoop, calls=%fused_computation.11 | loop fusion | flops 255 | bytes 513 | tf_op jit(solution)/shard_map/jit(cholesky)/cholesky | solution.py:31
  15.0 0.7 %fusion = f32[1,128,128]{2,1,0:T(8,128)S(1)} fusion(f32[128,128]{1,0:T(8,128)S(1)} %cholesky.16, pred[]{:T(512)} %compare_reduce_fusion), kind=kLoop, calls=%fused_computation.3 | loop fusion | flops 65536 | bytes 131073 | tf_op jit(solution)/shard_map/triangular_solve | solution.py:13
  15.7 9.8 %custom-call.6 = f32[1,128,128]{1,2,0:T(8,128)S(1)} custom-call(f32[1,128,128]{2,1,0:T(8,128)S(1)} %fusion), custom_call_target="InvertDiagBlocksLowerTriangular" | custom-call | tf_op jit(solution)/shard_map/triangular_solve | solution.py:13
  25.5 0.0 copy-done
  25.5 0.3 fusion.3
  25.8 0.8 %copy.14 = f32[256,128]{1,0:T(8,128)} copy(f32[256,128]{0,1:T(8,128)S(1)} %get-tuple-element.11) | data formatting | bytes 262144
  26.6 16.5 %all_gather.7 = bf16[2048,128]{0,1:T(8,128)(2,1)S(1)} all-gather(bf16[256,128]{0,1:T(8,128)(2,1)S(1)} %get-tuple-element.10), channel_id=1, replica_groups=mesh['prow'=4,'pcol'=8] {'pcol'}, dimensions={0}, use_global_device_ids=true | all-gather | bytes 589824 | tf_op jit(solution)/shard_map/all_gather | solution.py:38
  43.1 0.1 copy.11
  43.2 0.1 copy.12
  43.4 9.0 %all_gather.8 = bf16[4,256,128]{2,1,0:T(8,128)(2,1)S(1)} all-gather(bf16[1,256,128]{2,1,0:T(8,128)(2,1)S(1)} %maximum_select_fusion), channel_id=1, replica_groups=mesh['prow'=4,'pcol'=8] {'prow'}, dimensions={0}, use_global_device_ids=true | all-gather | bytes 327680 | tf_op jit(solution)/shard_map/all_gather | solution.py:9
  52.4 0.0 copy-done.1
  52.4 1.8 %convolution_subtract_fusion = f32[2048,256]{1,0:T(8,128)} fusion(f32[2048,256]{1,0:T(8,128)S(1)} %copy-done.1, bf16[2048,128]{0,1:T(8,128)(2,1)S(1)} %all_gather.7, bf16[256,128]{1,0:T(8,128)(2,1)S(1)} %reduce_sum.12), kind=kOutput, calls=%fused_computation | convolution fusion | flops 134742016 | bytes 4784128 | tf_op jit(solution)/shard_map/dot_general | solution.py:41
  (4 shorter events, 0.1 us)
Async XLA Ops:
  0.6 24.9 %copy-start = (f32[256,128]{1,0:T(8,128)S(1)}, f32[256,128]{1,0:T(8,128)}, u32[]{:S(2)}) copy-start(f32[256,128]{1,0:T(8,128)} %param.4) | copy-start | bytes 393220
  0.6 51.8 %copy-start.1 = (f32[2048,256]{1,0:T(8,128)S(1)}, f32[2048,256]{1,0:T(8,128)}, u32[]{:S(2)}) copy-start(f32[2048,256]{1,0:T(8,128)} %param.5) | copy-start | bytes 6291460
